TPU v7x, 32 devices: a whole 2x2x4 slice. The times are simulated.
32 devices in a mesh: rows: 8 (over z, x), width: 4 (over y, core).
Axes of the slice: x: 2, y: 2, z: 4, core: 2. Of those that a mesh axis runs over, the one named last changes fastest.
Arguments:
- queries: bfloat16 [6144, 4096], P('rows', 'width')
- passages: bfloat16 [2048, 4096], P('rows', 'width')
- neighbor_ids: int32 [24, 4], P('rows'), may hold values from 0 to 7, as said below
- counts: int32 [24], P('rows'), may hold values from 1 to 4
Outputs:
- losses: float32 [6144], P(('rows', 'width'))
- grad_queries: bfloat16 [6144, 4096], P('rows', 'width')
- grad_passages: bfloat16 [2048, 4096], P('rows', 'width')
Inputs may be any that keep to these rules, and one draw needn't show every extreme that they name: `neighbor_ids`: entry k of row c, for k below counts[c], names a passage block one or two blocks away from block c // 3 in the cyclic order of 8 blocks, all different within the row; the remaining entries name block c // 3.
All inputs are finite; a program needn't handle non-finite values.
Results may differ from a plain program's by a relative error of at most 0.0049.
Values may be sent and summed in bfloat16 or wider, within the bound.
A program may use at most 64 MiB of HBM per device.

v0:
```python
import jax
import jax.numpy as jnp
from jax import lax
from jax.sharding import PartitionSpec as P

BLOCK = 256


inverse_sharpness_scale = 50.0


def passed_along(block, axis, distance):
    devices = range(lax.axis_size(axis))
    route = [((i - distance) % len(devices), i) for i in devices]
    return lax.ppermute(block, axis, route)


def block_mask(neighbor_rows, count_rows, owner, nblocks):
    listed = jnp.arange(neighbor_rows.shape[1], dtype=jnp.int32)[None, :] < count_rows[:, None]
    columns = []
    for offset in range(5):
        if offset == 2:
            columns.append(jnp.ones((neighbor_rows.shape[0],), dtype=bool))
        else:
            target = (owner + offset - 2 + nblocks) % nblocks
            columns.append(jnp.any(listed & (neighbor_rows == target), axis=1))
    return jnp.stack(columns, axis=1)


def score_grads(pairwise_logits, row_exists_flag, local_rows):
    width_block = pairwise_logits.shape[1] // 5
    column_mask = jnp.repeat(row_exists_flag, width_block, axis=1)
    masked = jnp.where(column_mask, pairwise_logits, -jnp.inf)
    row_max = jnp.max(masked, axis=1, keepdims=True)
    expon = jnp.exp(masked - row_max)
    row_sum = jnp.sum(expon, axis=1, keepdims=True)
    normalized_probability = expon / row_sum
    positive_col = 2 * width_block + local_rows % width_block
    matching_pair_mask = (
        jnp.arange(pairwise_logits.shape[1], dtype=jnp.int32)[None, :] == positive_col[:, None]
    )
    positive = jnp.sum(jnp.where(matching_pair_mask, pairwise_logits, 0.0), axis=1)
    losses = row_max[:, 0] + jnp.log(row_sum[:, 0]) - positive
    derivative_entries = (
        inverse_sharpness_scale * (normalized_probability - matching_pair_mask.astype(jnp.float32))
    ).astype(jnp.bfloat16)
    return (losses, derivative_entries)


def per_device(queries, passages, neighbor_ids, counts):
    nblocks = lax.axis_size("rows")
    owner = lax.axis_index("rows")
    per_dev = queries.shape[0]
    present = block_mask(neighbor_ids, counts, owner, nblocks)
    fetched = []
    for offset in range(5):
        if offset == 2:
            fetched.append(passages)
        else:
            fetched.append(passed_along(passages, "rows", 2 - offset))
    candidates = jnp.concatenate(fetched, axis=0)
    score_dims = (((1,), (1,)), ((), ()))
    quantity_proportion = lax.dot_general(
        queries, candidates, score_dims, preferred_element_type=jnp.float32
    )
    row_exists_flag = jnp.repeat(present, BLOCK, axis=0)
    share_rows = per_dev // lax.axis_size("width")
    share_start = lax.axis_index("width") * share_rows
    pairwise_logits = lax.psum(quantity_proportion, "width") * inverse_sharpness_scale
    all_losses, derivative_entries = score_grads(
        pairwise_logits, row_exists_flag, jnp.arange(per_dev, dtype=jnp.int32)
    )
    losses = lax.dynamic_slice_in_dim(all_losses, share_start, share_rows, 0)
    grad_q = jnp.dot(derivative_entries, candidates, preferred_element_type=jnp.float32)
    passage_terms = lax.dot_general(
        derivative_entries, queries, (((0,), (0,)), ((), ())), preferred_element_type=jnp.float32
    )
    term_sums = [passage_terms[offset * BLOCK : (offset + 1) * BLOCK] for offset in range(5)]
    total = term_sums[2]
    for offset in (0, 1, 3, 4):
        arrived = passed_along(term_sums[offset].astype(jnp.bfloat16), "rows", offset - 2)
        total = total + arrived.astype(jnp.float32)
    return (losses, grad_q.astype(jnp.bfloat16), total.astype(jnp.bfloat16))


def solution(mesh):
    return jax.shard_map(
        per_device,
        mesh=mesh,
        in_specs=(P("rows", "width"), P("rows", "width"), P("rows", None), P("rows")),
        out_specs=(P(("rows", "width")), P("rows", "width"), P("rows", "width")),
        check_vma=False,
    )
```

profile of v0, /device:TPU:0, one launch (start us, length us, event | category | flops | bytes accessed | tf_op | source)
XLA Modules:
  0.0 190.1 jit_solution(16085234565629834959)
XLA Ops:
  7.2 0.0 copy-start
  7.2 0.0 all-reduce.2.cloned.1.call-start
  7.2 3.1 %collective-permute-start = (bf16[256,1024]{1,0:T(8,128)(2,1)}, bf16[256,1024]{1,0:T(8,128)(2,1)S(1)}, u32[]{:S(2)}, u32[]{:S(2)}) collective-permute-start(bf16[256,1024]{1,0:T(8,128)(2,1)} %param.5), channel_id=1, source_target_pairs={{24,0},{28,4},{0,8},{4,12},{8,16},{12,20},{16,24},{20,28},{25,1},{... | collective-permute-start | bytes 1572872 | tf_op jit(solution)/shard_map/ppermute | solution.py:15
  10.3 1.5 collective-permute-start.1
  11.8 3.2 %collective-permute-start.2 = (bf16[256,1024]{1,0:T(8,128)(2,1)}, bf16[256,1024]{1,0:T(8,128)(2,1)S(1)}, u32[]{:S(2)}, u32[]{:S(2)}) collective-permute-start(bf16[256,1024]{1,0:T(8,128)(2,1)} %param.5), channel_id=1, source_target_pairs={{4,0},{8,4},{12,8},{16,12},{20,16},{24,20},{28,24},{0,28},{5,1},{9... | collective-permute-start | bytes 1572872 | tf_op jit(solution)/shard_map/ppermute | solution.py:15
  15.0 0.3 collective-permute-start.3
  15.3 10.0 %collective-permute-done = bf16[256,1024]{1,0:T(8,128)(2,1)S(1)} collective-permute-done((bf16[256,1024]{1,0:T(8,128)(2,1)}, bf16[256,1024]{1,0:T(8,128)(2,1)S(1)}, u32[]{:S(2)}, u32[]{:S(2)}) %collective-permute-start) | collective-permute-done | bytes 524320 | tf_op jit(solution)/shard_map/ppermute | solution.py:15
  25.4 12.4 %collective-permute-done.1 = bf16[256,1024]{1,0:T(8,128)(2,1)S(1)} collective-permute-done((bf16[256,1024]{1,0:T(8,128)(2,1)}, bf16[256,1024]{1,0:T(8,128)(2,1)S(1)}, u32[]{:S(2)}, u32[]{:S(2)}) %collective-permute-start.1) | collective-permute-done | bytes 524320 | tf_op jit(solution)/shard_map/ppermute | solution.py:15
  37.8 1.1 constant_dynamic-update-slice_fusion.2
  38.9 0.0 collective-permute-done.2
  38.9 8.0 %collective-permute-done.3 = bf16[256,1024]{1,0:T(8,128)(2,1)S(1)} collective-permute-done((bf16[256,1024]{1,0:T(8,128)(2,1)}, bf16[256,1024]{1,0:T(8,128)(2,1)S(1)}, u32[]{:S(2)}, u32[]{:S(2)}) %collective-permute-start.3) | collective-permute-done | bytes 524320 | tf_op jit(solution)/shard_map/ppermute | solution.py:15
  47.0 0.0 copy-start.2
  47.0 1.6 copy-done.2
  48.5 0.0 copy-done
  48.5 4.1 %convolution_bitcast_fusion = f32[768,1280]{0,1:T(8,128)} fusion(bf16[1280,1024]{1,0:T(8,128)(2,1)S(1)} %constant_dynamic-update-slice_fusion, bf16[768,1024]{1,0:T(8,128)(2,1)S(1)} %copy-done), kind=kOutput, calls=%fused_computation.5 | convolution fusion | flops 2013265920 | bytes 8126464 | tf_op jit(solution)/shard_map/dot_general | solution.py:63
  52.7 0.0 copy-start.4
  52.7 0.0 copy-start.5
  52.7 0.0 all-reduce.2.cloned.1.call-update
  52.8 0.6 copy-done.4
  53.4 0.0 copy-done.5
  53.4 0.2 fusion.17
  53.6 0.1 broadcast_bitcast_fusion
  53.7 81.0 %all-reduce.2.cloned.1.call-done = f32[768,1280]{0,1:T(8,128)} async-done(((f32[768,1280]{0,1:T(8,128)}), f32[768,1280]{0,1:T(8,128)}) %all-reduce.2.cloned.1.call-update) | async-done | bytes 3932176 | tf_op jit(solution)/shard_map/psum | solution.py:69
  134.7 0.0 copy-start.1
  134.7 2.7 %fusion = f32[768]{0:T(1024)S(1)} fusion(f32[768,1280]{0,1:T(8,128)} %all-reduce.2.cloned.1.call-done, pred[768,5]{0,1:T(8,128)(4,1)S(1)} %bitcast.27), kind=kLoop, calls=%fused_computation.6 | loop fusion | flops 2948352 | bytes 3939072 | tf_op jit(solution)/shard_map/reduce_max | solution.py:34
  137.4 0.6 copy-done.1
  138.0 1.3 fusion.1
  139.3 1.5 multiply_convert_fusion
  140.8 2.2 %fusion.19 = (bf16[1280,1024]{1,0:T(8,128)(2,1)S(1)}, f32[1280,1024]{1,0:T(8,128)S(1)}) fusion(bf16[768,1280]{0,1:T(8,128)(2,1)S(1)} %multiply_convert_fusion, bf16[768,1024]{1,0:T(8,128)(2,1)S(1)} %copy-done), kind=kOutput, calls=%fused_computation.37 | convolution fusion | flops 2014576640 | bytes 11403264 | tf_op jit(solution)/shard_map/dot_general | solution.py:75
  143.0 0.0 copy-start.3
  143.0 0.2 fusion.18
  143.2 3.4 %collective-permute-start.4 = (bf16[256,1024]{1,0:T(8,128)(2,1)S(1)}, bf16[256,1024]{1,0:T(8,128)(2,1)S(1)}, u32[]{:S(2)}, u32[]{:S(2)}) collective-permute-start(bf16[256,1024]{1,0:T(8,128)(2,1)S(1)} %get-tuple-element.9), channel_id=1, source_target_pairs={{8,0},{12,4},{16,8},{20,12},{24,16},{28,20},{0,24},{4,28},{9,1},{1... | collective-permute-start | bytes 1572872 | tf_op jit(solution)/shard_map/ppermute | solution.py:15
  146.6 0.0 collective-permute-start.7
  146.6 1.5 collective-permute-start.6
  148.1 3.3 %collective-permute-start.5 = (bf16[256,1024]{1,0:T(8,128)(2,1)S(1)}, bf16[256,1024]{1,0:T(8,128)(2,1)S(1)}, u32[]{:S(2)}, u32[]{:S(2)}) collective-permute-start(bf16[256,1024]{1,0:T(8,128)(2,1)S(1)} %get-tuple-element.12), channel_id=1, source_target_pairs={{4,0},{8,4},{12,8},{16,12},{20,16},{24,20},{28,24},{0,28},{5,1},{9... | collective-permute-start | bytes 1572872 | tf_op jit(solution)/shard_map/ppermute | solution.py:15
  151.3 0.6 dynamic_slice.3
  152.0 0.0 copy-done.3
  152.0 3.4 %convolution_convert_fusion = bf16[768,1024]{1,0:T(8,128)(2,1)} fusion(bf16[768,1280]{0,1:T(8,128)(2,1)S(1)} %multiply_convert_fusion, bf16[1280,1024]{1,0:T(8,128)(2,1)S(1)} %copy-done.3), kind=kOutput, calls=%fused_computation.8 | convolution fusion | flops 2014052352 | bytes 6160384 | tf_op jit(solution)/shard_map/dot_general | solution.py:74
  155.4 3.6 %collective-permute-done.4 = bf16[256,1024]{1,0:T(8,128)(2,1)S(1)} collective-permute-done((bf16[256,1024]{1,0:T(8,128)(2,1)S(1)}, bf16[256,1024]{1,0:T(8,128)(2,1)S(1)}, u32[]{:S(2)}, u32[]{:S(2)}) %collective-permute-start.4) | collective-permute-done | bytes 524320 | tf_op jit(solution)/shard_map/ppermute | solution.py:15
  158.9 12.3 %collective-permute-done.7 = bf16[256,1024]{1,0:T(8,128)(2,1)S(1)} collective-permute-done((bf16[256,1024]{1,0:T(8,128)(2,1)S(1)}, bf16[256,1024]{1,0:T(8,128)(2,1)S(1)}, u32[]{:S(2)}, u32[]{:S(2)}) %collective-permute-start.7) | collective-permute-done | bytes 524320 | tf_op jit(solution)/shard_map/ppermute | solution.py:15
  171.2 10.8 %collective-permute-done.6 = bf16[256,1024]{1,0:T(8,128)(2,1)S(1)} collective-permute-done((bf16[256,1024]{1,0:T(8,128)(2,1)S(1)}, bf16[256,1024]{1,0:T(8,128)(2,1)S(1)}, u32[]{:S(2)}, u32[]{:S(2)}) %collective-permute-start.6) | collective-permute-done | bytes 524320 | tf_op jit(solution)/shard_map/ppermute | solution.py:15
  182.0 0.0 collective-permute-done.5
  182.0 1.3 fusion.5
  (9 shorter events, 0.2 us)
Async XLA Ops:
  7.2 41.4 %copy-start = (bf16[768,1024]{1,0:T(8,128)(2,1)S(1)}, bf16[768,1024]{1,0:T(8,128)(2,1)}, u32[]{:S(2)}) copy-start(bf16[768,1024]{1,0:T(8,128)(2,1)} %param.4) | copy-start | bytes 4718596
  7.2 127.5 %all-reduce.2.cloned.1.call-start = ((), (), s32[]{:S(2)}) async-start(), calls=%async_computation | async-start | bytes 7864320 | tf_op jit(solution)/shard_map/psum | solution.py:69
  7.2 18.1 %collective-permute-start = (bf16[256,1024]{1,0:T(8,128)(2,1)}, bf16[256,1024]{1,0:T(8,128)(2,1)S(1)}, u32[]{:S(2)}, u32[]{:S(2)}) collective-permute-start(bf16[256,1024]{1,0:T(8,128)(2,1)} %param.5), channel_id=1, source_target_pairs={{24,0},{28,4},{0,8},{4,12},{8,16},{12,20},{16,24},{20,28},{25,1},{... | collective-permute-start | bytes 1572872 | tf_op jit(solution)/shard_map/ppermute | solution.py:15
  10.3 27.4 %collective-permute-start.1 = (bf16[256,1024]{1,0:T(8,128)(2,1)}, bf16[256,1024]{1,0:T(8,128)(2,1)S(1)}, u32[]{:S(2)}, u32[]{:S(2)}) collective-permute-start(bf16[256,1024]{1,0:T(8,128)(2,1)} %param.5), channel_id=1, source_target_pairs={{28,0},{0,4},{4,8},{8,12},{12,16},{16,20},{20,24},{24,28},{29,1},{... | collective-permute-start | bytes 1572872 | tf_op jit(solution)/shard_map/ppermute | solution.py:15
  11.8 27.1 %collective-permute-start.2 = (bf16[256,1024]{1,0:T(8,128)(2,1)}, bf16[256,1024]{1,0:T(8,128)(2,1)S(1)}, u32[]{:S(2)}, u32[]{:S(2)}) collective-permute-start(bf16[256,1024]{1,0:T(8,128)(2,1)} %param.5), channel_id=1, source_target_pairs={{4,0},{8,4},{12,8},{16,12},{20,16},{24,20},{28,24},{0,28},{5,1},{9... | collective-permute-start | bytes 1572872 | tf_op jit(solution)/shard_map/ppermute | solution.py:15
  15.0 31.9 %collective-permute-start.3 = (bf16[256,1024]{1,0:T(8,128)(2,1)}, bf16[256,1024]{1,0:T(8,128)(2,1)S(1)}, u32[]{:S(2)}, u32[]{:S(2)}) collective-permute-start(bf16[256,1024]{1,0:T(8,128)(2,1)} %param.5), channel_id=1, source_target_pairs={{8,0},{12,4},{16,8},{20,12},{24,16},{28,20},{0,24},{4,28},{9,1},{1... | collective-permute-start | bytes 1572872 | tf_op jit(solution)/shard_map/ppermute | solution.py:15
  47.0 1.6 copy-start.2
  52.7 0.7 copy-start.4
  52.7 0.7 copy-start.5
  134.7 3.3 %copy-start.1 = (f32[768,1280]{0,1:T(8,128)S(1)}, f32[768,1280]{0,1:T(8,128)}, u32[]{:S(2)}) copy-start(f32[768,1280]{0,1:T(8,128)} %all-reduce.2.cloned.1.call-done) | copy-start | bytes 11796484
  143.0 8.9 %copy-start.3 = (bf16[1280,1024]{1,0:T(8,128)(2,1)S(1)}, bf16[1280,1024]{1,0:T(8,128)(2,1)}, u32[]{:S(2)}) copy-start(bf16[1280,1024]{1,0:T(8,128)(2,1)} %copy-done.2) | copy-start | bytes 7864324
  143.2 15.7 %collective-permute-start.4 = (bf16[256,1024]{1,0:T(8,128)(2,1)S(1)}, bf16[256,1024]{1,0:T(8,128)(2,1)S(1)}, u32[]{:S(2)}, u32[]{:S(2)}) collective-permute-start(bf16[256,1024]{1,0:T(8,128)(2,1)S(1)} %get-tuple-element.9), channel_id=1, source_target_pairs={{8,0},{12,4},{16,8},{20,12},{24,16},{28,20},{0,24},{4,28},{9,1},{1... | collective-permute-start | bytes 1572872 | tf_op jit(solution)/shard_map/ppermute | solution.py:15
  146.6 24.6 %collective-permute-start.7 = (bf16[256,1024]{1,0:T(8,128)(2,1)S(1)}, bf16[256,1024]{1,0:T(8,128)(2,1)S(1)}, u32[]{:S(2)}, u32[]{:S(2)}) collective-permute-start(bf16[256,1024]{1,0:T(8,128)(2,1)S(1)} %get-tuple-element.10), channel_id=1, source_target_pairs={{24,0},{28,4},{0,8},{4,12},{8,16},{12,20},{16,24},{20,28},{25,1},{... | collective-permute-start | bytes 1572872 | tf_op jit(solution)/shard_map/ppermute | solution.py:15
  146.6 35.4 %collective-permute-start.6 = (bf16[256,1024]{1,0:T(8,128)(2,1)S(1)}, bf16[256,1024]{1,0:T(8,128)(2,1)S(1)}, u32[]{:S(2)}, u32[]{:S(2)}) collective-permute-start(bf16[256,1024]{1,0:T(8,128)(2,1)S(1)} %get-tuple-element.11), channel_id=1, source_target_pairs={{28,0},{0,4},{4,8},{8,12},{12,16},{16,20},{20,24},{24,28},{29,1},{... | collective-permute-start | bytes 1572872 | tf_op jit(solution)/shard_map/ppermute | solution.py:15
  148.1 33.9 %collective-permute-start.5 = (bf16[256,1024]{1,0:T(8,128)(2,1)S(1)}, bf16[256,1024]{1,0:T(8,128)(2,1)S(1)}, u32[]{:S(2)}, u32[]{:S(2)}) collective-permute-start(bf16[256,1024]{1,0:T(8,128)(2,1)S(1)} %get-tuple-element.12), channel_id=1, source_target_pairs={{4,0},{8,4},{12,8},{16,12},{20,16},{24,20},{28,24},{0,28},{5,1},{9... | collective-permute-start | bytes 1572872 | tf_op jit(solution)/shard_map/ppermute | solution.py:15
Sparse Core Ops, SparseCore 0:
  52.8 81.8 all-reduce.1
where the time goes:
time: 190 us
  waiting for transfers between devices  138 us (73%)
  starting transfers between devices  16.2 us (9%)
  between operations  14.2 us (7%)
  matrix products  9.76 us (5%)
  other arithmetic  6.98 us (4%)
  local copies, waits for them, and re-layouts  4.91 us (3%)
    psum x1, waiting for transfers between devices, per_device(): lax.psum(quantity_proportion, 'width') * inverse_sharpness_scale  81 us
    ppermute x8, waiting for transfers between devices, passed_along(): return lax.ppermute(block, axis, route)  57 us
    ppermute x8, starting transfers between devices, passed_along(): return lax.ppermute(block, axis, route)  16.2 us
    dot_general x1, matrix products, per_device(): lax.dot_general(queries, candidates, score_dims, preferred_element_type=j...  4.15 us
    unnamed x18, local copies, waits for them, and re-layouts  4.03 us
  transfers between devices with their start and end apart: 9, of which 7 were waited for; matrix products, arithmetic and copies ran while one was open for 3% of the time, Pallas kernels for 0%

commit v1 on v0

v1 whole, which is shorter than its diff:
```python
import functools

import jax
import jax.numpy as jnp
from jax import lax
from jax.experimental import pallas as pl
from jax.experimental.pallas import tpu as pltpu
from jax.sharding import PartitionSpec as P

MESH = pl.DeviceIdType.MESH
SCALE = 50.0
PIECES = 2
OWN, AHEAD, BEHIND, PAIR, RELAY = 0, 1, 2, 3, 4
SLOTS = 5
RETURN_ORDER = (RELAY, BEHIND, AHEAD, PAIR, OWN)

NT = (((1,), (1,)), ((), ()))
TN = (((0,), (0,)), ((), ()))
NN = (((1,), (0,)), ((), ()))


def dot(a, b, dims):
    return lax.dot_general(a, b, dims, preferred_element_type=jnp.float32)


def copies_needed():
    gather = 4 * PIECES
    scores = SLOTS * 3
    grads = SLOTS * 3
    terms = 4 * PIECES
    return gather + scores + grads + terms


def kernel(
    nrows, ids_ref, counts_ref, q_ref, p_ref, loss_ref, gq_ref, gp_ref,
    pbuf, spart, rs1, rs2s, rs2r, gbuf, lossbuf, term_own, term_ahead,
    tsend, trecv, send_sem, recv_sem,
):
    r = lax.axis_index("rows")
    w = lax.axis_index("width")
    par = lax.rem(r, 2)
    step = 2 - 4 * par
    pair = r + 1 - 2 * par
    ahead = lax.rem(r + step + nrows, nrows)
    behind = lax.rem(r - step + nrows, nrows)
    core = lax.rem(w, 2)
    side = w + 1 - 2 * core
    across = lax.rem(w + 2, 4)
    diagonal = lax.rem(side + 2, 4)
    block, width = p_ref.shape
    share = q_ref.shape[0] // 4

    to_pair, to_ahead, to_behind = {"rows": pair}, {"rows": ahead}, {"rows": behind}
    to_side, to_across = {"width": side}, {"width": across}

    barrier = pltpu.get_barrier_semaphore()
    for device in (to_pair, to_ahead, to_behind, to_side, to_across):
        pl.semaphore_signal(barrier, inc=1, device_id=device, device_id_type=MESH)
    pl.semaphore_wait(barrier, 5)

    started = []

    def send(src, dst, device):
        n = len(started)
        copy = pltpu.make_async_remote_copy(
            src_ref=src, dst_ref=dst, send_sem=send_sem.at[n], recv_sem=recv_sem.at[n],
            device_id=device, device_id_type=MESH,
        )
        copy.start()
        started.append(copy)
        return copy

    rows_piece = block // PIECES
    piece = [pl.ds(k * rows_piece, rows_piece) for k in range(PIECES)]
    arrive = {AHEAD: [], BEHIND: [], PAIR: [], RELAY: []}
    for k in range(PIECES):
        arrive[AHEAD].append(send(p_ref.at[piece[k]], pbuf.at[AHEAD - 1, piece[k]], to_behind))
        arrive[PAIR].append(send(p_ref.at[piece[k]], pbuf.at[PAIR - 1, piece[k]], to_pair))
        arrive[BEHIND].append(send(p_ref.at[piece[k]], pbuf.at[BEHIND - 1, piece[k]], to_ahead))

    def candidates(slot):
        return p_ref if slot == OWN else pbuf.at[slot - 1]

    first, second = {}, {}

    def score_block(slot):
        part = dot(q_ref[...], candidates(slot)[...], NT)
        spart[slot] = part.reshape(4, share, block)
        far = send(spart.at[slot, diagonal], rs1.at[slot, 1], to_side)
        near = send(spart.at[slot, side], rs1.at[slot, 0], to_side)
        first[slot] = (far, near)

    def score_pass_on(slot):
        first[slot][0].wait_recv()
        rs2s[slot] = spart[slot, across] + rs1[slot, 1]
        second[slot] = send(rs2s.at[slot], rs2r.at[slot], to_across)

    score_block(OWN)
    score_pass_on(OWN)
    for k in range(PIECES):
        arrive[PAIR][k].wait_recv()
    score_block(PAIR)
    for k in range(PIECES):
        arrive[AHEAD][k].wait_recv()
        arrive[RELAY].append(
            send(pbuf.at[AHEAD - 1, piece[k]], pbuf.at[RELAY - 1, piece[k]], to_pair))
    score_pass_on(PAIR)
    score_block(AHEAD)
    score_pass_on(AHEAD)
    for k in range(PIECES):
        arrive[BEHIND][k].wait_recv()
    score_block(BEHIND)
    score_pass_on(BEHIND)
    for k in range(PIECES):
        arrive[RELAY][k].wait_recv()
    score_block(RELAY)
    score_pass_on(RELAY)

    offsets = (0, step, -step, pair - r, r - pair)
    targets = [lax.rem(r + offset + nrows, nrows) for offset in offsets]
    nblk = ids_ref.shape[0]
    present = []
    for slot in range(1, SLOTS):
        flags = []
        for c in range(nblk):
            flag = jnp.int32(0)
            for k in range(ids_ref.shape[1]):
                hit = jnp.logical_and(k < counts_ref[c], ids_ref[c, k] == targets[slot])
                flag = jnp.maximum(flag, jnp.where(hit, jnp.int32(1), jnp.int32(0)))
            flags.append(flag)
        present.append(flags)

    for slot in range(SLOTS):
        first[slot][1].wait_recv()
        second[slot].wait_recv()

    tile = 32

    @pl.loop(0, share // tile)
    def _(i):
        at = pl.ds(pl.multiple_of(i * tile, tile), tile)
        row = w * share + i * tile + lax.broadcasted_iota(jnp.int32, (tile, block), 0)
        col = lax.broadcasted_iota(jnp.int32, (tile, block), 1)
        is_pos = col == lax.rem(row, block)
        which = row // block
        logits = []
        for slot in range(SLOTS):
            s = (spart[slot, w, at] + rs1[slot, 0, at] + rs2r[slot, at]) * SCALE
            if slot != OWN:
                flags = present[slot - 1]
                on = jnp.full((tile, block), flags[0], jnp.int32)
                for c in range(1, nblk):
                    on = jnp.where(which == c, flags[c], on)
                s = jnp.where(on > 0, s, -jnp.inf)
            logits.append(s)
        top = functools.reduce(jnp.maximum, logits)
        top = jnp.max(top, axis=1, keepdims=True)
        expon = [jnp.exp(s - top) for s in logits]
        total = jnp.sum(functools.reduce(jnp.add, expon), axis=1, keepdims=True)
        positive = jnp.sum(jnp.where(is_pos, logits[OWN], 0.0), axis=1, keepdims=True)
        loss = top + jnp.log(total) - positive
        lossbuf[at] = jnp.broadcast_to(loss, (tile, lossbuf.shape[1]))
        for slot in range(SLOTS):
            weight = expon[slot] / total
            if slot == OWN:
                weight = weight - jnp.where(is_pos, 1.0, 0.0)
            gbuf[slot, w, at] = (SCALE * weight).astype(jnp.bfloat16)

    from_across, from_side, from_diagonal = {}, {}, {}
    for slot in RETURN_ORDER:
        from_across[slot] = send(gbuf.at[slot, w], gbuf.at[slot, w], to_across)
        from_side[slot] = send(gbuf.at[slot, w], gbuf.at[slot, w], to_side)

    n = lossbuf.shape[1]
    eye = (lax.broadcasted_iota(jnp.int32, (share, n), 0)
           == lax.broadcasted_iota(jnp.int32, (share, n), 1))
    loss_ref[...] = jnp.sum(jnp.where(eye, lossbuf[...], 0.0), axis=0, keepdims=True)[:, :share]

    cols = width // PIECES
    merged = {}
    for slot in RETURN_ORDER:
        from_across[slot].wait_recv()
        from_diagonal[slot] = send(gbuf.at[slot, across], gbuf.at[slot, across], to_side)
        from_side[slot].wait_recv()
        from_diagonal[slot].wait_recv()
        grads = gbuf[slot].reshape(4 * share, block)
        for k in range(PIECES):
            term = dot(grads, q_ref[:, k * cols:(k + 1) * cols], TN)
            if slot == OWN:
                term_own[k] = term
            elif slot == AHEAD:
                term_ahead[k] = term
            else:
                tsend[slot - 1, k] = term.astype(jnp.bfloat16)
                device = to_behind if slot == BEHIND else to_pair
                merged[slot, k] = send(tsend.at[slot - 1, k], trecv.at[slot - 1, k], device)
    for k in range(PIECES):
        merged[RELAY, k].wait_recv()
        both = term_ahead[k] + trecv[RELAY - 1, k].astype(jnp.float32)
        tsend[AHEAD - 1, k] = both.astype(jnp.bfloat16)
        merged[AHEAD, k] = send(tsend.at[AHEAD - 1, k], trecv.at[AHEAD - 1, k], to_ahead)

    tile_cols = 256

    @pl.loop(0, width // tile_cols)
    def _(j):
        at = pl.ds(pl.multiple_of(j * tile_cols, tile_cols), tile_cols)
        total = dot(gbuf[OWN].reshape(4 * share, block), p_ref[:, at], NN)
        for slot in range(1, SLOTS):
            total += dot(gbuf[slot].reshape(4 * share, block), pbuf[slot - 1, :, at], NN)
        gq_ref[:, at] = total.astype(jnp.bfloat16)

    for k in range(PIECES):
        total = term_own[k]
        for slot in (PAIR, BEHIND, AHEAD):
            merged[slot, k].wait_recv()
            total += trecv[slot - 1, k].astype(jnp.float32)
        gp_ref[:, k * cols:(k + 1) * cols] = total.astype(jnp.bfloat16)

    for copy in started:
        copy.wait_send()


def per_device(queries, passages, neighbor_ids, counts):
    nrows = lax.axis_size("rows")
    assert lax.axis_size("width") == 4 and nrows % 2 == 0
    per_dev, width = queries.shape
    block = passages.shape[0]
    share = per_dev // 4
    lanes = -(-share // 128) * 128
    vmem = pl.BlockSpec(memory_space=pltpu.VMEM)
    smem = pl.BlockSpec(memory_space=pltpu.SMEM)
    bf16, f32 = jnp.bfloat16, jnp.float32
    ncopies = copies_needed()
    losses, grad_q, grad_p = pl.pallas_call(
        functools.partial(kernel, nrows),
        out_shape=(
            jax.ShapeDtypeStruct((1, share), f32),
            jax.ShapeDtypeStruct((per_dev, width), bf16),
            jax.ShapeDtypeStruct((block, width), bf16),
        ),
        in_specs=[smem, smem, vmem, vmem],
        out_specs=(vmem, vmem, vmem),
        scratch_shapes=[
            pltpu.VMEM((SLOTS - 1, block, width), bf16),
            pltpu.VMEM((SLOTS, 4, share, block), f32),
            pltpu.VMEM((SLOTS, 2, share, block), f32),
            pltpu.VMEM((SLOTS, share, block), f32),
            pltpu.VMEM((SLOTS, share, block), f32),
            pltpu.VMEM((SLOTS, 4, share, block), bf16),
            pltpu.VMEM((share, lanes), f32),
            pltpu.VMEM((PIECES, block, width // PIECES), f32),
            pltpu.VMEM((PIECES, block, width // PIECES), f32),
            pltpu.VMEM((SLOTS - 1, PIECES, block, width // PIECES), bf16),
            pltpu.VMEM((SLOTS - 1, PIECES, block, width // PIECES), bf16),
            pltpu.SemaphoreType.DMA((ncopies,)),
            pltpu.SemaphoreType.DMA((ncopies,)),
        ],
        compiler_params=pltpu.CompilerParams(
            collective_id=0, has_side_effects=True, vmem_limit_bytes=50 * 1024 * 1024
        ),
    )(neighbor_ids, counts, queries, passages)
    return losses.reshape(share), grad_q, grad_p


def solution(mesh):
    return jax.shard_map(
        per_device,
        mesh=mesh,
        in_specs=(P("rows", "width"), P("rows", "width"), P("rows", None), P("rows")),
        out_specs=(P(("rows", "width")), P("rows", "width"), P("rows", "width")),
        check_vma=False,
    )
```

time: 190 us -> 85.9 us (0.45)
  waiting for transfers between devices: 138 us -> 0 us
  Pallas kernels: 0 us -> 80.2 us
  starting transfers between devices: 16.2 us -> 0 us
  between operations: 14.2 us -> 0.65 us
  matrix products: 9.76 us -> 0 us
  other arithmetic: 6.98 us -> 0 us
    psum x1 -> x0, waiting for transfers between devices: 81 us -> none  [per_device(): lax.psum(quantity_proportion, 'width') * inverse_sharpness_scale]
    pallas_call x0 -> x1, Pallas kernels: none -> 80.2 us  [per_device(): pl.pallas_call(functools.partial(kernel, nrows), out_shape=(jax.ShapeDtyp...]
    ppermute x8 -> x0, waiting for transfers between devices: 57 us -> none  [passed_along(): return lax.ppermute(block, axis, route)]
    ppermute x8 -> x0, starting transfers between devices: 16.2 us -> none  [passed_along(): return lax.ppermute(block, axis, route)]
    dot_general x3 -> x0, matrix products: 9.76 us -> none  [the longest x1 4.15 us: per_device(): lax.dot_general(queries, candidates, score_dims, preferred_element_type=j...]
    reduce_max x1 -> x0, other arithmetic: 2.73 us -> none  [score_grads(): row_max = jnp.max(masked, axis=1, keepdims=True)]
    convert_element_type x2 -> x0, other arithmetic: 2.72 us -> none  [the longest x1 1.47 us: score_grads(): derivative_entries = (inverse_sharpness_scale * (normalized_probability -...]
    unnamed x18 -> x9, local copies, waits for them, and re-layouts: 4.03 us -> 4.87 us
  transfers between devices with their start and end apart: 9 -> 0, of which waited for: 7 -> 0; matrix products, arithmetic and copies ran while one was open for 3% -> 0% of each run, Pallas kernels for 0% -> 0%
where the time goes in v1:
time: 85.9 us; the launch traced here: 85.7 us
  Pallas kernels  80.2 us (93%)
  local copies, waits for them, and re-layouts  4.87 us (6%)
    pallas_call x1, Pallas kernels, per_device(): pl.pallas_call(functools.partial(kernel, nrows), out_shape=(jax.ShapeDtyp...  80.2 us
    unnamed x9, local copies, waits for them, and re-layouts  4.87 us

profile of v1, /device:TPU:0, one launch (start us, length us, event | category | flops | bytes accessed | tf_op | source)
XLA Modules:
  0.0 85.7 jit_solution(12276527657424708273)
XLA Ops:
  0.6 0.0 copy-start
  0.6 1.0 %copy-done = bf16[256,1024]{1,0:T(8,128)(2,1)S(1)} copy-done((bf16[256,1024]{1,0:T(8,128)(2,1)S(1)}, bf16[256,1024]{1,0:T(8,128)(2,1)}, u32[]{:S(2)}) %copy-start) | copy-done | bytes 524312
  1.7 0.0 copy-start.1
  1.7 0.7 copy-done.1
  2.4 0.0 copy-start.2
  2.4 0.7 copy-done.2
  3.0 80.2 %shard_map.67 = (f32[1,192]{1,0:T(1,128)S(1)}, bf16[768,1024]{1,0:T(8,128)(2,1)S(1)}, bf16[256,1024]{1,0:T(8,128)(2,1)S(1)}) custom-call(s32[3,4]{1,0:T(4,128)S(1)} %copy-done.1, s32[3]{0:T(128)S(1)} %copy-done.2, bf16[768,1024]{1,0:T(8,128)(2,1)} %q_ref.1, bf16[256,1024]{1,0:T(8,128)(2,1)S(1)} %copy-done), custom_call_target="tpu_custom_call" | custom-call | tf_op jit(solution)/shard_map/pallas_call | solution.py:235
  83.2 0.6 copy.10
  83.8 1.1 %copy.11 = bf16[768,1024]{1,0:T(8,128)(2,1)} copy(bf16[768,1024]{1,0:T(8,128)(2,1)S(1)} %get-tuple-element.13) | data formatting | bytes 3145728
  84.9 0.8 copy.12
Async XLA Ops:
  0.6 1.0 %copy-start = (bf16[256,1024]{1,0:T(8,128)(2,1)S(1)}, bf16[256,1024]{1,0:T(8,128)(2,1)}, u32[]{:S(2)}) copy-start(bf16[256,1024]{1,0:T(8,128)(2,1)} %p_ref.1) | copy-start | bytes 1572868
  1.7 0.7 copy-start.1
  2.4 0.7 copy-start.2

commit v2 on v1

v2 whole, which is shorter than its diff:
```python
import functools

import jax
import jax.numpy as jnp
from jax import lax
from jax.experimental import pallas as pl
from jax.experimental.pallas import tpu as pltpu
from jax.sharding import PartitionSpec as P

MESH = pl.DeviceIdType.MESH
SCALE = 50.0
PIECES = 2
OWN, AHEAD, BEHIND, PAIR, RELAY = 0, 1, 2, 3, 4
SLOTS = 5
RETURN_ORDER = (
    (RELAY, 0), (BEHIND, 0), (RELAY, 1), (BEHIND, 1), (AHEAD, 0), (PAIR, 0), (AHEAD, 1), (PAIR, 1),
    (OWN, 0), (OWN, 1),
)

NT = (((1,), (1,)), ((), ()))
TN = (((0,), (0,)), ((), ()))
NN = (((1,), (0,)), ((), ()))


def dot(a, b, dims):
    return lax.dot_general(a, b, dims, preferred_element_type=jnp.float32)


def copies_needed():
    gather = 4 * PIECES
    scores = SLOTS * PIECES * 3
    grads = SLOTS * PIECES * 3
    terms = 4 * PIECES
    return gather + scores + grads + terms


def kernel(
    nrows, lists_hbm, q_hbm, p_hbm, loss_ref, gq_ref, gp_ref,
    pbuf, spart, rs1, rs2s, rs2r, gbuf, lossbuf, term_own, term_ahead,
    tsend, trecv, lists_ref, q_ref, p_ref, local_sem, send_sem, recv_sem,
):
    r = lax.axis_index("rows")
    w = lax.axis_index("width")
    par = lax.rem(r, 2)
    step = 2 - 4 * par
    pair = r + 1 - 2 * par
    ahead = lax.rem(r + step + nrows, nrows)
    behind = lax.rem(r - step + nrows, nrows)
    core = lax.rem(w, 2)
    side = w + 1 - 2 * core
    across = lax.rem(w + 2, 4)
    diagonal = lax.rem(side + 2, 4)
    block, width = p_ref.shape
    share = q_ref.shape[0] // 4

    to_pair, to_ahead, to_behind = {"rows": pair}, {"rows": ahead}, {"rows": behind}
    to_side, to_across = {"width": side}, {"width": across}

    local = [
        pltpu.make_async_copy(src, dst, local_sem.at[n])
        for n, (src, dst) in enumerate((
            (p_hbm, p_ref), (q_hbm, q_ref), (lists_hbm, lists_ref)))
    ]
    for copy in local:
        copy.start()

    barrier = pltpu.get_barrier_semaphore()
    for device in (to_pair, to_ahead, to_behind, to_side, to_across):
        pl.semaphore_signal(barrier, inc=1, device_id=device, device_id_type=MESH)
    pl.semaphore_wait(barrier, 5)

    started = []

    def send(src, dst, device):
        n = len(started)
        copy = pltpu.make_async_remote_copy(
            src_ref=src, dst_ref=dst, send_sem=send_sem.at[n], recv_sem=recv_sem.at[n],
            device_id=device, device_id_type=MESH,
        )
        copy.start()
        started.append(copy)
        return copy

    unit = block // PIECES
    piece = [pl.ds(k * unit, unit) for k in range(PIECES)]
    arrive = {}

    def pass_block(slot, k, src, device):
        arrive[slot, k] = send(src.at[piece[k]], pbuf.at[slot - 1, piece[k]], device)

    for k in range(PIECES):
        pass_block(AHEAD, k, p_hbm, to_behind)
        pass_block(PAIR, k, p_hbm, to_pair)
    sent = []

    def behind(k):
        arrive[AHEAD, k].wait_send()
        sent.append(id(arrive[AHEAD, k]))
        pass_block(BEHIND, k, p_hbm, to_ahead)

    def relay(k):
        arrive[AHEAD, k].wait_recv()
        pass_block(RELAY, k, pbuf.at[AHEAD - 1], to_pair)

    first, second, pending = {}, {}, []

    def pass_on():
        slot, k = pending.pop(0)
        first[slot, k][0].wait_recv()
        rs2s[slot, k] = spart[slot, k, across] + rs1[slot, k, 1]
        second[slot, k] = send(rs2s.at[slot, k], rs2r.at[slot, k], to_across)

    def score(slot, k):
        if slot in (PAIR, BEHIND, RELAY):
            arrive[slot, k].wait_recv()
        rows = p_ref[piece[k]] if slot == OWN else pbuf[slot - 1, piece[k]]
        spart[slot, k] = dot(q_ref[...], rows, NT).reshape(4, share, unit)
        first[slot, k] = (
            send(spart.at[slot, k, diagonal], rs1.at[slot, k, 1], to_side),
            send(spart.at[slot, k, side], rs1.at[slot, k, 0], to_side),
        )
        pending.append((slot, k))
        if len(pending) > 1:
            pass_on()

    for copy in local:
        copy.wait()
    for k in range(PIECES):
        score(OWN, k)
    for k in range(PIECES):
        behind(k)
        relay(k)
        score(PAIR, k)
        score(AHEAD, k)
    for k in range(PIECES):
        score(BEHIND, k)
        score(RELAY, k)
    pass_on()

    offsets = (0, step, -step, pair - r, r - pair)
    targets = [lax.rem(r + offset + nrows, nrows) for offset in offsets]
    nblk, nslots = lists_ref.shape[0], lists_ref.shape[1] - 1
    present = []
    for slot in range(1, SLOTS):
        flags = []
        for c in range(nblk):
            flag = jnp.int32(0)
            for k in range(nslots):
                hit = jnp.logical_and(k < lists_ref[c, nslots], lists_ref[c, k] == targets[slot])
                flag = jnp.maximum(flag, jnp.where(hit, jnp.int32(1), jnp.int32(0)))
            flags.append(flag)
        present.append(flags)

    for key in first:
        first[key][1].wait_recv()
        second[key].wait_recv()

    tile = 32
    keys = [(slot, k) for slot in range(SLOTS) for k in range(PIECES)]

    @pl.loop(0, share // tile)
    def _(i):
        at = pl.ds(pl.multiple_of(i * tile, tile), tile)
        row = w * share + i * tile + lax.broadcasted_iota(jnp.int32, (tile, unit), 0)
        col = lax.broadcasted_iota(jnp.int32, (tile, unit), 1)
        pos = lax.rem(row, block)
        which = row // block
        masks = []
        for flags in present:
            on = jnp.full((tile, unit), flags[0], jnp.int32)
            for c in range(1, nblk):
                on = jnp.where(which == c, flags[c], on)
            masks.append(on > 0)
        logits, positives = [], []
        for slot, k in keys:
            s = (spart[slot, k, w, at] + rs1[slot, k, 0, at] + rs2r[slot, k, at]) * SCALE
            if slot == OWN:
                positives.append(jnp.where(col + k * unit == pos, s, 0.0))
            else:
                s = jnp.where(masks[slot - 1], s, -jnp.inf)
            logits.append(s)
        top = jnp.max(functools.reduce(jnp.maximum, logits), axis=1, keepdims=True)
        expon = [jnp.exp(s - top) for s in logits]
        total = jnp.sum(functools.reduce(jnp.add, expon), axis=1, keepdims=True)
        positive = jnp.sum(functools.reduce(jnp.add, positives), axis=1, keepdims=True)
        loss = top + jnp.log(total) - positive
        lossbuf[at] = jnp.broadcast_to(loss, (tile, lossbuf.shape[1]))
        factor = SCALE / total
        for (slot, k), e in zip(keys, expon):
            g = e * factor
            if slot == OWN:
                g = g - jnp.where(col + k * unit == pos, SCALE, 0.0)
            gbuf[slot, k, w, at] = g.astype(jnp.bfloat16)

    from_across, from_side, from_diagonal = {}, {}, {}
    for slot, k in RETURN_ORDER:
        mine = gbuf.at[slot, k, w]
        from_across[slot, k] = send(mine, mine, to_across)
        from_side[slot, k] = send(mine, mine, to_side)

    n = lossbuf.shape[1]
    eye = (lax.broadcasted_iota(jnp.int32, (share, n), 0)
           == lax.broadcasted_iota(jnp.int32, (share, n), 1))
    loss_ref[...] = jnp.sum(jnp.where(eye, lossbuf[...], 0.0), axis=0, keepdims=True)[:, :share]

    merged = {}
    tiles = 2
    cols = width // tiles

    def relay_grads(slot, k):
        from_across[slot, k].wait_recv()
        other = gbuf.at[slot, k, across]
        from_diagonal[slot, k] = send(other, other, to_side)

    def term_piece(slot, k):
        from_side[slot, k].wait_recv()
        from_diagonal[slot, k].wait_recv()
        grads = gbuf[slot, k].reshape(4 * share, unit)
        for j in range(tiles):
            at = slice(j * cols, (j + 1) * cols)
            term = dot(grads, q_ref[:, at], TN)
            if slot == OWN:
                term_own[piece[k], at] = term
            elif slot == AHEAD:
                term_ahead[piece[k], at] = term
            else:
                tsend[slot - 1, piece[k], at] = term.astype(jnp.bfloat16)
        if slot not in (OWN, AHEAD):
            device = to_behind if slot == BEHIND else to_pair
            merged[slot, k] = send(
                tsend.at[slot - 1, piece[k]], trecv.at[slot - 1, piece[k]], device)

    relay_grads(*RETURN_ORDER[0])
    for here, later in zip(RETURN_ORDER, RETURN_ORDER[1:] + (None,)):
        term_piece(*here)
        if later is not None:
            relay_grads(*later)
    for k in range(PIECES):
        merged[RELAY, k].wait_recv()
        both = term_ahead[piece[k]] + trecv[RELAY - 1, piece[k]].astype(jnp.float32)
        tsend[AHEAD - 1, piece[k]] = both.astype(jnp.bfloat16)
        merged[AHEAD, k] = send(
            tsend.at[AHEAD - 1, piece[k]], trecv.at[AHEAD - 1, piece[k]], to_ahead)

    tile_cols = 256

    @pl.loop(0, width // tile_cols)
    def _(j):
        at = pl.ds(pl.multiple_of(j * tile_cols, tile_cols), tile_cols)
        total = None
        for slot in range(SLOTS):
            for k in range(PIECES):
                rows = p_ref[piece[k], at] if slot == OWN else pbuf[slot - 1, piece[k], at]
                part = dot(gbuf[slot, k].reshape(4 * share, unit), rows, NN)
                total = part if total is None else total + part
        gq_ref[:, at] = total.astype(jnp.bfloat16)

    for k in range(PIECES):
        total = term_own[piece[k]]
        for slot in (PAIR, BEHIND, AHEAD):
            merged[slot, k].wait_recv()
            total += trecv[slot - 1, piece[k]].astype(jnp.float32)
        gp_ref[piece[k]] = total.astype(jnp.bfloat16)

    for copy in started:
        if id(copy) not in sent:
            copy.wait_send()


def store_kernel(*refs):
    *pairs, sems = refs
    half = len(pairs) // 2
    copies = [
        pltpu.make_async_copy(src, dst, sems.at[n])
        for n, (src, dst) in enumerate(zip(pairs[:half], pairs[half:]))
    ]
    for copy in copies:
        copy.start()
    for copy in copies:
        copy.wait()


def store(*arrays):
    return pl.pallas_call(
        store_kernel,
        out_shape=tuple(jax.ShapeDtypeStruct(a.shape, a.dtype) for a in arrays),
        in_specs=[pl.BlockSpec(memory_space=pl.ANY)] * len(arrays),
        out_specs=tuple(pl.BlockSpec(memory_space=pltpu.HBM) for a in arrays),
        scratch_shapes=[pltpu.SemaphoreType.DMA((len(arrays),))],
        compiler_params=pltpu.CompilerParams(vmem_limit_bytes=2 * 1024 * 1024),
    )(*arrays)


def per_device(queries, passages, neighbor_ids, counts):
    nrows = lax.axis_size("rows")
    assert lax.axis_size("width") == 4 and nrows % 2 == 0
    per_dev, width = queries.shape
    block = passages.shape[0]
    share = per_dev // 4
    unit = block // PIECES
    lanes = -(-share // 128) * 128
    vmem = pl.BlockSpec(memory_space=pltpu.VMEM)
    hbm = pl.BlockSpec(memory_space=pltpu.HBM)
    bf16, f32 = jnp.bfloat16, jnp.float32
    ncopies = copies_needed()
    lists = jnp.concatenate([neighbor_ids, counts[:, None]], axis=1)
    results = pl.pallas_call(
        functools.partial(kernel, nrows),
        out_shape=(
            jax.ShapeDtypeStruct((1, share), f32),
            jax.ShapeDtypeStruct((per_dev, width), bf16),
            jax.ShapeDtypeStruct((block, width), bf16),
        ),
        in_specs=[hbm, hbm, hbm],
        out_specs=(vmem, vmem, vmem),
        scratch_shapes=[
            pltpu.VMEM((SLOTS - 1, block, width), bf16),
            pltpu.VMEM((SLOTS, PIECES, 4, share, unit), f32),
            pltpu.VMEM((SLOTS, PIECES, 2, share, unit), f32),
            pltpu.VMEM((SLOTS, PIECES, share, unit), f32),
            pltpu.VMEM((SLOTS, PIECES, share, unit), f32),
            pltpu.VMEM((SLOTS, PIECES, 4, share, unit), bf16),
            pltpu.VMEM((share, lanes), f32),
            pltpu.VMEM((block, width), f32),
            pltpu.VMEM((block, width), f32),
            pltpu.VMEM((SLOTS - 1, block, width), bf16),
            pltpu.VMEM((SLOTS - 1, block, width), bf16),
            pltpu.SMEM(lists.shape, jnp.int32),
            pltpu.VMEM((per_dev, width), bf16),
            pltpu.VMEM((block, width), bf16),
            pltpu.SemaphoreType.DMA((3,)),
            pltpu.SemaphoreType.DMA((ncopies,)),
            pltpu.SemaphoreType.DMA((ncopies,)),
        ],
        compiler_params=pltpu.CompilerParams(
            collective_id=0, has_side_effects=True, vmem_limit_bytes=50 * 1024 * 1024
        ),
    )(lists, queries, passages)
    losses, grad_q, grad_p = store(*results)
    return losses.reshape(share), grad_q, grad_p


def solution(mesh):
    return jax.shard_map(
        per_device,
        mesh=mesh,
        in_specs=(P("rows", "width"), P("rows", "width"), P("rows", None), P("rows")),
        out_specs=(P(("rows", "width")), P("rows", "width"), P("rows", "width")),
        check_vma=False,
    )
```

time: 85.9 us -> 78.3 us (0.912)
  Pallas kernels: 80.2 us -> 74.9 us
  local copies, waits for them, and re-layouts: 4.87 us -> 1.78 us
    pallas_call x1, Pallas kernels: 80.2 us -> 73.5 us  [per_device(): pl.pallas_call(functools.partial(kernel, nrows), out_shape=(jax.ShapeDtyp...]
    unnamed x9 -> x2, local copies, waits for them, and re-layouts: 4.87 us -> 1.04 us
    pallas_call x0 -> x1, Pallas kernels: none -> 1.34 us  [store(): pl.pallas_call(store_kernel, out_shape=tuple((jax.ShapeDtypeStruct(a.shap...]
where the time goes in v2:
time: 78.3 us; the launch traced here: 78.1 us
  Pallas kernels  74.9 us (96%)
  local copies, waits for them, and re-layouts  1.78 us (2%)
    pallas_call x1, Pallas kernels, per_device(): pl.pallas_call(functools.partial(kernel, nrows), out_shape=(jax.ShapeDtyp...  73.5 us

profile of v2, /device:TPU:0, one launch (start us, length us, event | category | flops | bytes accessed | tf_op | source)
XLA Modules:
  0.0 78.1 jit_solution(16393095438545085027)
XLA Ops:
  0.6 0.7 copy.7
  1.4 0.8 pad_add_fusion.lists_hbm
  2.1 0.0 copy-start
  2.1 1.0 %copy-done = bf16[256,1024]{1,0:T(8,128)(2,1)S(1)} copy-done((bf16[256,1024]{1,0:T(8,128)(2,1)S(1)}, bf16[256,1024]{1,0:T(8,128)(2,1)}, u32[]{:S(2)}) %copy-start) | copy-done | bytes 524312
  3.2 73.5 %shard_map.67 = (f32[1,192]{1,0:T(1,128)S(1)}, bf16[768,1024]{1,0:T(8,128)(2,1)S(1)}, bf16[256,1024]{1,0:T(8,128)(2,1)S(1)}) custom-call(s32[3,5]{1,0:T(4,128)S(1)} %pad_add_fusion.lists_hbm, bf16[768,1024]{1,0:T(8,128)(2,1)} %q_hbm.1, bf16[256,1024]{1,0:T(8,128)(2,1)S(1)} %copy-done), custom_call_target="tpu_custom_call" | custom-call | tf_op jit(solution)/shard_map/pallas_call | solution.py:307
  76.7 1.3 %shard_map.68 = (f32[1,192]{1,0:T(1,128)}, bf16[768,1024]{1,0:T(8,128)(2,1)}, bf16[256,1024]{1,0:T(8,128)(2,1)}) custom-call(f32[1,192]{1,0:T(1,128)S(1)} %get-tuple-element.9.refs_0_, bf16[768,1024]{1,0:T(8,128)(2,1)S(1)} %get-tuple-element.10.refs_1_, bf16[256,1024]{1,0:T(8,128)(2,1)S(1)} %get-tuple-element.11.refs_2_), custom_call_target="tpu_custom_call" | custom-call | tf_op jit(solution)/shard_map/pallas_call | solution.py:284
Async XLA Ops:
  2.1 1.0 %copy-start = (bf16[256,1024]{1,0:T(8,128)(2,1)S(1)}, bf16[256,1024]{1,0:T(8,128)(2,1)}, u32[]{:S(2)}) copy-start(bf16[256,1024]{1,0:T(8,128)(2,1)} %p_hbm.1) | copy-start | bytes 1572868

commit v3 on v2

--- a/solution.py
+++ b/solution.py
@@ -27,7 +27,7 @@
 
 
 def copies_needed():
-    gather = 4 * PIECES
+    gather = 6 * PIECES
     scores = SLOTS * PIECES * 3
     grads = SLOTS * PIECES * 3
     terms = 4 * PIECES
@@ -85,8 +85,15 @@
     piece = [pl.ds(k * unit, unit) for k in range(PIECES)]
     arrive = {}
 
+    small = unit // 2
+    strip = [pl.ds(m * small, small) for m in range(2 * PIECES)]
+
     def pass_block(slot, k, src, device):
         arrive[slot, k] = send(src.at[piece[k]], pbuf.at[slot - 1, piece[k]], device)
+
+    def pass_strips(slot, k, src, device):
+        for m in (2 * k, 2 * k + 1):
+            arrive[slot, m] = send(src.at[strip[m]], pbuf.at[slot - 1, strip[m]], device)
 
     for k in range(PIECES):
         pass_block(AHEAD, k, p_hbm, to_behind)
@@ -96,11 +103,11 @@
     def behind(k):
         arrive[AHEAD, k].wait_send()
         sent.append(id(arrive[AHEAD, k]))
-        pass_block(BEHIND, k, p_hbm, to_ahead)
+        pass_strips(BEHIND, k, p_hbm, to_ahead)
 
     def relay(k):
         arrive[AHEAD, k].wait_recv()
-        pass_block(RELAY, k, pbuf.at[AHEAD - 1], to_pair)
+        pass_strips(RELAY, k, pbuf.at[AHEAD - 1], to_pair)
 
     first, second, pending = {}, {}, []
 
@@ -111,9 +118,18 @@
         second[slot, k] = send(rs2s.at[slot, k], rs2r.at[slot, k], to_across)
 
     def score(slot, k):
-        if slot in (PAIR, BEHIND, RELAY):
-            arrive[slot, k].wait_recv()
-        rows = p_ref[piece[k]] if slot == OWN else pbuf[slot - 1, piece[k]]
+        if slot in (BEHIND, RELAY):
+            m = 2 * k + (slot == RELAY)
+            arrive[BEHIND, m].wait_recv()
+            arrive[RELAY, m].wait_recv()
+            rows = jnp.concatenate(
+                [pbuf[BEHIND - 1, strip[m]], pbuf[RELAY - 1, strip[m]]], axis=0)
+        elif slot == OWN:
+            rows = p_ref[piece[k]]
+        else:
+            if slot == PAIR:
+                arrive[PAIR, k].wait_recv()
+            rows = pbuf[slot - 1, piece[k]]
         spart[slot, k] = dot(q_ref[...], rows, NT).reshape(4, share, unit)
         first[slot, k] = (
             send(spart.at[slot, k, diagonal], rs1.at[slot, k, 1], to_side),
@@ -158,6 +174,13 @@
     tile = 32
     keys = [(slot, k) for slot in range(SLOTS) for k in range(PIECES)]
 
+    def flags_of(slot, which):
+        flags = present[slot - 1]
+        on = jnp.full((tile, unit), flags[0], jnp.int32)
+        for c in range(1, nblk):
+            on = jnp.where(which == c, flags[c], on)
+        return on
+
     @pl.loop(0, share // tile)
     def _(i):
         at = pl.ds(pl.multiple_of(i * tile, tile), tile)
@@ -165,12 +188,11 @@
         col = lax.broadcasted_iota(jnp.int32, (tile, unit), 1)
         pos = lax.rem(row, block)
         which = row // block
-        masks = []
-        for flags in present:
-            on = jnp.full((tile, unit), flags[0], jnp.int32)
-            for c in range(1, nblk):
-                on = jnp.where(which == c, flags[c], on)
-            masks.append(on > 0)
+        masks = [flags_of(slot, which) > 0 for slot in range(1, SLOTS)]
+        left = col < small
+        mixed = jnp.where(
+            left, flags_of(BEHIND, which), flags_of(RELAY, which)) > 0
+        masks[BEHIND - 1] = masks[RELAY - 1] = mixed
         logits, positives = [], []
         for slot, k in keys:
             s = (spart[slot, k, w, at] + rs1[slot, k, 0, at] + rs2r[slot, k, at]) * SCALE
@@ -186,8 +208,13 @@
         loss = top + jnp.log(total) - positive
         lossbuf[at] = jnp.broadcast_to(loss, (tile, lossbuf.shape[1]))
         factor = SCALE / total
-        for (slot, k), e in zip(keys, expon):
-            g = e * factor
+        grads = {key: e * factor for key, e in zip(keys, expon)}
+        for k in range(PIECES):
+            one, two = grads[BEHIND, k], grads[RELAY, k]
+            grads[BEHIND, k] = jnp.concatenate([one[:, :small], two[:, :small]], axis=1)
+            grads[RELAY, k] = jnp.concatenate([one[:, small:], two[:, small:]], axis=1)
+        for slot, k in keys:
+            g = grads[slot, k]
             if slot == OWN:
                 g = g - jnp.where(col + k * unit == pos, SCALE, 0.0)
             gbuf[slot, k, w, at] = g.astype(jnp.bfloat16)

time: 78.3 us -> 76.8 us (0.981)
  Pallas kernels: 74.9 us -> 73.4 us
    pallas_call x1, Pallas kernels: 73.5 us -> 72.1 us  [per_device(): pl.pallas_call(functools.partial(kernel, nrows), out_shape=(jax.ShapeDtyp...]
where the time goes in v3:
time: 76.8 us; the launch traced here: 76.6 us
  Pallas kernels  73.4 us (96%)
  local copies, waits for them, and re-layouts  1.78 us (2%)
    pallas_call x1, Pallas kernels, per_device(): pl.pallas_call(functools.partial(kernel, nrows), out_shape=(jax.ShapeDtyp...  72.1 us

profile of v3, /device:TPU:0, one launch (start us, length us, event | category | flops | bytes accessed | tf_op | source)
XLA Modules:
  0.0 76.6 jit_solution(8809030401301080460)
XLA Ops:
  0.6 0.7 copy.7
  1.4 0.8 pad_add_fusion.lists_hbm
  2.1 0.0 copy-start
  2.1 1.0 %copy-done = bf16[256,1024]{1,0:T(8,128)(2,1)S(1)} copy-done((bf16[256,1024]{1,0:T(8,128)(2,1)S(1)}, bf16[256,1024]{1,0:T(8,128)(2,1)}, u32[]{:S(2)}) %copy-start) | copy-done | bytes 524312
  3.2 72.1 %shard_map.67 = (f32[1,192]{1,0:T(1,128)S(1)}, bf16[768,1024]{1,0:T(8,128)(2,1)S(1)}, bf16[256,1024]{1,0:T(8,128)(2,1)S(1)}) custom-call(s32[3,5]{1,0:T(4,128)S(1)} %pad_add_fusion.lists_hbm, bf16[768,1024]{1,0:T(8,128)(2,1)} %q_hbm.1, bf16[256,1024]{1,0:T(8,128)(2,1)S(1)} %copy-done), custom_call_target="tpu_custom_call" | custom-call | tf_op jit(solution)/shard_map/pallas_call | solution.py:334
  75.3 1.3 %shard_map.68 = (f32[1,192]{1,0:T(1,128)}, bf16[768,1024]{1,0:T(8,128)(2,1)}, bf16[256,1024]{1,0:T(8,128)(2,1)}) custom-call(f32[1,192]{1,0:T(1,128)S(1)} %get-tuple-element.9.refs_0_, bf16[768,1024]{1,0:T(8,128)(2,1)S(1)} %get-tuple-element.10.refs_1_, bf16[256,1024]{1,0:T(8,128)(2,1)S(1)} %get-tuple-element.11.refs_2_), custom_call_target="tpu_custom_call" | custom-call | tf_op jit(solution)/shard_map/pallas_call | solution.py:311
Async XLA Ops:
  2.1 1.0 %copy-start = (bf16[256,1024]{1,0:T(8,128)(2,1)S(1)}, bf16[256,1024]{1,0:T(8,128)(2,1)}, u32[]{:S(2)}) copy-start(bf16[256,1024]{1,0:T(8,128)(2,1)} %p_hbm.1) | copy-start | bytes 1572868

commit v4 on v3

--- a/solution.py
+++ b/solution.py
@@ -181,7 +181,7 @@
             on = jnp.where(which == c, flags[c], on)
         return on
 
-    @pl.loop(0, share // tile)
+    @pl.loop(0, share // tile, unroll=2)
     def _(i):
         at = pl.ds(pl.multiple_of(i * tile, tile), tile)
         row = w * share + i * tile + lax.broadcasted_iota(jnp.int32, (tile, unit), 0)
@@ -257,17 +257,22 @@
             merged[slot, k] = send(
                 tsend.at[slot - 1, piece[k]], trecv.at[slot - 1, piece[k]], device)
 
+    def merge(k):
+        merged[RELAY, k].wait_recv()
+        both = term_ahead[piece[k]] + trecv[RELAY - 1, piece[k]].astype(jnp.float32)
+        tsend[AHEAD - 1, piece[k]] = both.astype(jnp.bfloat16)
+        merged[AHEAD, k] = send(
+            tsend.at[AHEAD - 1, piece[k]], trecv.at[AHEAD - 1, piece[k]], to_ahead)
+
     relay_grads(*RETURN_ORDER[0])
     for here, later in zip(RETURN_ORDER, RETURN_ORDER[1:] + (None,)):
         term_piece(*here)
         if later is not None:
             relay_grads(*later)
-    for k in range(PIECES):
-        merged[RELAY, k].wait_recv()
-        both = term_ahead[piece[k]] + trecv[RELAY - 1, piece[k]].astype(jnp.float32)
-        tsend[AHEAD - 1, piece[k]] = both.astype(jnp.bfloat16)
-        merged[AHEAD, k] = send(
-            tsend.at[AHEAD - 1, piece[k]], trecv.at[AHEAD - 1, piece[k]], to_ahead)
+        if here == (PAIR, PIECES - 1):
+            merge(0)
+    for k in range(1, PIECES):
+        merge(k)
 
     tile_cols = 256
 

time: 76.8 us -> 76 us (0.990)
  Pallas kernels: 73.4 us -> 72.6 us
    pallas_call x1, Pallas kernels: 72.1 us -> 71.3 us  [per_device(): pl.pallas_call(functools.partial(kernel, nrows), out_shape=(jax.ShapeDtyp...]
where the time goes in v4:
time: 76 us; the launch traced here: 75.8 us
  Pallas kernels  72.6 us (96%)
  local copies, waits for them, and re-layouts  1.78 us (2%)
    pallas_call x1, Pallas kernels, per_device(): pl.pallas_call(functools.partial(kernel, nrows), out_shape=(jax.ShapeDtyp...  71.3 us

profile of v4, /device:TPU:0, one launch (start us, length us, event | category | flops | bytes accessed | tf_op | source)
XLA Modules:
  0.0 75.8 jit_solution(5492482041356503472)
XLA Ops:
  0.6 0.7 copy.7
  1.4 0.8 pad_add_fusion.lists_hbm
  2.1 0.0 copy-start
  2.1 1.0 %copy-done = bf16[256,1024]{1,0:T(8,128)(2,1)S(1)} copy-done((bf16[256,1024]{1,0:T(8,128)(2,1)S(1)}, bf16[256,1024]{1,0:T(8,128)(2,1)}, u32[]{:S(2)}) %copy-start) | copy-done | bytes 524312
  3.2 71.3 %shard_map.67 = (f32[1,192]{1,0:T(1,128)S(1)}, bf16[768,1024]{1,0:T(8,128)(2,1)S(1)}, bf16[256,1024]{1,0:T(8,128)(2,1)S(1)}) custom-call(s32[3,5]{1,0:T(4,128)S(1)} %pad_add_fusion.lists_hbm, bf16[768,1024]{1,0:T(8,128)(2,1)} %q_hbm.1, bf16[256,1024]{1,0:T(8,128)(2,1)S(1)} %copy-done), custom_call_target="tpu_custom_call" | custom-call | tf_op jit(solution)/shard_map/pallas_call | solution.py:339
  74.5 1.3 %shard_map.68 = (f32[1,192]{1,0:T(1,128)}, bf16[768,1024]{1,0:T(8,128)(2,1)}, bf16[256,1024]{1,0:T(8,128)(2,1)}) custom-call(f32[1,192]{1,0:T(1,128)S(1)} %get-tuple-element.9.refs_0_, bf16[768,1024]{1,0:T(8,128)(2,1)S(1)} %get-tuple-element.10.refs_1_, bf16[256,1024]{1,0:T(8,128)(2,1)S(1)} %get-tuple-element.11.refs_2_), custom_call_target="tpu_custom_call" | custom-call | tf_op jit(solution)/shard_map/pallas_call | solution.py:316
Async XLA Ops:
  2.1 1.0 %copy-start = (bf16[256,1024]{1,0:T(8,128)(2,1)S(1)}, bf16[256,1024]{1,0:T(8,128)(2,1)}, u32[]{:S(2)}) copy-start(bf16[256,1024]{1,0:T(8,128)(2,1)} %p_hbm.1) | copy-start | bytes 1572868
